TPU v7x, 256 devices: a whole 4x4x8 slice. The times are simulated.
256 devices in a mesh: samp: 64 (over z, x, y_lo), snp: 4 (over y_hi, core).
Axes of the slice: x: 4, y: 4 (y_hi: 2, y_lo: 2; y = y_hi * 2 + y_lo), z: 8, core: 2. Of those that a mesh axis runs over, the one named last changes fastest.
Arguments:
- genotypes: bfloat16 [32768, 16384], P('samp', 'snp'), may hold values from 0 to 2, as said below
- traits: bfloat16 [32768, 256], P('samp'), may hold values from -40 to 40
- trait_basis: float32 [256, 64], replicated, may hold values from -0.375 to 0.375
Outputs:
- fitted: bfloat16 [32768, 256], P('samp')
- covariance: float32 [256, 256], replicated
- scores: float32 [32768, 64], P('samp')
Inputs may be any that keep to these rules, and one draw needn't show every extreme that they name: `genotypes`: every entry is a whole number of alleles: 0, 1 or 2.
All inputs are finite; a program needn't handle non-finite values.
Results may differ from a plain program's by a relative error of at most 0.0044.
Values may be sent and summed in bfloat16 or wider, within the bound.
A program may use at most 64 MiB of HBM per device.

v0:
```python
import jax
import jax.numpy as jnp
from jax import lax
from jax.sharding import PartitionSpec as P


def local(genotypes, traits, trait_basis):
    highest = lax.Precision.HIGHEST
    sample_rows = genotypes.shape[0]
    snp_columns = genotypes.shape[1]
    trait_count = traits.shape[1]
    groups = lax.axis_size("samp")
    all_samples = sample_rows * groups
    ridge_weight = all_samples / 8.0
    share_rows = snp_columns // groups
    geno_mean = lax.psum(jnp.sum(genotypes, axis=0, dtype=jnp.float32), "samp") / all_samples
    trait_local = jnp.sum(traits, axis=0, dtype=jnp.float32)
    product = lax.dot_general(
        genotypes, traits, (((0,), (0,)), ((), ())), preferred_element_type=jnp.float32
    )
    normal = lax.psum(product - geno_mean[:, None] * trait_local[None, :], "samp")
    own_start = lax.axis_index("samp") * share_rows
    own_rows = lax.dynamic_slice_in_dim(normal, own_start, share_rows, 0)
    norm_part = jnp.sum(own_rows * own_rows, axis=0)
    normal_bf = normal.astype(jnp.bfloat16)
    projected = jnp.dot(genotypes, normal_bf, preferred_element_type=jnp.float32)
    shifted = jnp.dot(geno_mean, normal_bf.astype(jnp.float32), precision=highest)
    fitted_part = projected - shifted[None, :]
    fitted_raw, norm_snp = lax.psum((fitted_part, norm_part), "snp")
    gram_part = lax.dot_general(fitted_raw, fitted_raw, (((0,), (0,)), ((), ())), precision=highest)
    diag_sum, norm_sum = lax.psum((jnp.sum(fitted_raw * fitted_raw, axis=0), norm_snp), "samp")
    gram_sum = lax.psum(gram_part, "samp")
    step_size = norm_sum / (diag_sum + ridge_weight * norm_sum)
    fitted = (fitted_raw * step_size[None, :]).astype(jnp.bfloat16)
    covariance = step_size[:, None] * gram_sum * step_size[None, :] / all_samples
    loading = jnp.dot(covariance, trait_basis, precision=highest)
    spread = jnp.trace(covariance) + 1e-06
    scores = trait_count * jnp.dot(fitted.astype(jnp.float32), loading, precision=highest) / spread
    return (fitted, covariance, scores)


def solution(mesh):
    placed = (P("samp", "snp"), P("samp", None), P())
    return jax.shard_map(
        local,
        mesh=mesh,
        in_specs=placed,
        out_specs=(P("samp", None), P(), P("samp", None)),
        check_vma=False,
    )
```

profile of v0, /device:TPU:1, one launch (start us, length us, event | category | flops | bytes accessed | tf_op | source)
XLA Modules:
  0.0 1533.0 jit_solution(15106667465751133647)
XLA Ops:
  7.2 0.0 copy-start
  7.2 0.0 copy-start.3
  7.2 0.0 all-reduce.5.cloned.1.call-start
  7.2 3.2 convert_reduce_fusion
  10.5 257.1 %psum.49 = f32[4096]{0:T(1024)S(1)} all-reduce(f32[4096]{0:T(1024)S(1)} %convert_reduce_fusion), channel_id=1, replica_groups=mesh['samp'=64,'snp'=4] {'samp'}, use_global_device_ids=true, to_apply=%region_1.0 | all-reduce | flops 4096 | bytes 32768 | tf_op jit(solution)/shard_map/psum | solution.py:16
  267.6 0.0 copy-done.3
  267.6 0.1 convert_reduce_fusion.1
  267.7 5.9 convolution_subtract_fusion
  273.6 0.0 all-reduce.5.cloned.1.call-update
  273.6 0.0 all-reduce.7.cloned.1.call-start
  273.7 627.5 %all-reduce.5.cloned.1.call-done = f32[4096,256]{1,0:T(8,128)} async-done(((f32[4096,256]{1,0:T(8,128)}), f32[4096,256]{1,0:T(8,128)}) %all-reduce.5.cloned.1.call-update) | async-done | bytes 4194320 | tf_op jit(solution)/shard_map/psum | solution.py:21
  901.2 0.0 copy-start.1
  901.2 3.3 fusion.2
  904.4 0.2 copy-done.1
  904.6 4.4 fusion
  909.0 0.0 all-reduce.7.cloned.1.call-update
  909.0 0.0 all-reduce.9.cloned.1.call-start
  909.1 0.9 multiply_reduce_fusion.1
  910.0 49.9 %psum.52 = f32[256]{0:T(256)S(1)} all-reduce(f32[256]{0:T(256)S(1)} %multiply_reduce_fusion.1), channel_id=1, replica_groups=mesh['samp'=64,'snp'=4] {'snp'}, use_global_device_ids=true, to_apply=%region_6.0 | all-reduce | flops 256 | bytes 2048 | tf_op jit(solution)/shard_map/psum | solution.py:29
  959.9 37.2 %all-reduce.7.cloned.1.call-done = f32[512,256]{0,1:T(8,128)} async-done(((f32[512,256]{0,1:T(8,128)}), f32[512,256]{0,1:T(8,128)}) %all-reduce.7.cloned.1.call-update) | async-done | bytes 524304 | tf_op jit(solution)/shard_map/psum | solution.py:29
  997.0 2.5 fusion.5
  999.6 0.0 all-reduce.9.cloned.1.call-update
  999.6 1.2 multiply_reduce_fusion
  1000.7 131.5 %all-reduce = (f32[256]{0:T(256)S(1)}, f32[256]{0:T(256)S(1)}) all-reduce(f32[256]{0:T(256)S(1)} %psum.52, f32[256]{0:T(256)S(1)} %multiply_reduce_fusion), channel_id=1, replica_groups=mesh['samp'=64,'snp'=4] {'samp'}, use_global_device_ids=true, to_apply=%region_7.0 | all-reduce | flops 512 | bytes 4096 | tf_op jit(solution)/shard_map/psum | solution.py:31
  1132.3 1.1 multiply_convert_fusion
  1133.4 0.8 copy.6
  1134.3 388.5 %all-reduce.9.cloned.1.call-done = f32[256,256]{1,0:T(8,128)} async-done(((f32[256,256]{1,0:T(8,128)}), f32[256,256]{1,0:T(8,128)}) %all-reduce.9.cloned.1.call-update) | async-done | bytes 262160 | tf_op jit(solution)/shard_map/psum | solution.py:32
  1522.8 1.7 select_reduce_fusion
  1524.5 0.0 copy-start.2
  1524.5 0.0 copy-done
  1524.5 0.4 fusion.6
  1525.5 0.9 fusion.1
  1526.5 0.0 copy-done.2
  (2 shorter events, 0.0 us)
Async XLA Ops:
  7.2 1517.3 %copy-start = (f32[256,64]{0,1:T(8,128)S(1)}, f32[256,64]{0,1:T(8,128)}, u32[]{:S(2)}) copy-start(f32[256,64]{0,1:T(8,128)} %param.5) | copy-start | bytes 196612
  7.2 260.4 %copy-start.3 = (bf16[512,256]{1,0:T(8,128)(2,1)S(1)}, bf16[512,256]{1,0:T(8,128)(2,1)}, u32[]{:S(2)}) copy-start(bf16[512,256]{1,0:T(8,128)(2,1)} %param.4) | copy-start | bytes 786436
  7.2 894.0 %all-reduce.5.cloned.1.call-start = ((), (), s32[]{:S(2)}) async-start(), calls=%async_computation | async-start | bytes 8388608 | tf_op jit(solution)/shard_map/psum | solution.py:21
  273.6 723.4 %all-reduce.7.cloned.1.call-start = ((), (), s32[]{:S(2)}) async-start(), calls=%async_computation.1 | async-start | bytes 1048576 | tf_op jit(solution)/shard_map/psum | solution.py:29
  901.2 3.4 copy-start.1
  909.0 613.8 %all-reduce.9.cloned.1.call-start = ((), (), s32[]{:S(2)}) async-start(), calls=%async_computation.2 | async-start | bytes 524288 | tf_op jit(solution)/shard_map/psum | solution.py:32
  1524.5 2.0 copy-start.2
Sparse Core Ops, SparseCore 0:
  273.7 627.3 all-reduce.4
  909.1 87.8 all-reduce.6
  1000.4 522.3 all-reduce.8
where the time goes:
time: 1560 us; the launch traced here: 1530 us
  waiting for transfers between devices  1050 us (67%)
  blocking collectives  439 us (28%)
  matrix products  17.4 us (1%)
    psum x1, waiting for transfers between devices, local(): lax.psum(product - geno_mean[:, None] * trait_local[None, :], 'samp')  627 us
    psum x1, waiting for transfers between devices, local(): gram_sum = lax.psum(gram_part, 'samp')  389 us
    psum x1, blocking collectives, local(): lax.psum(jnp.sum(genotypes, axis=0, dtype=jnp.float32), 'samp')  257 us
    psum x1, blocking collectives, local(): lax.psum((jnp.sum(fitted_raw * fitted_raw, axis=0), norm_snp), 'samp')  132 us
    psum x1, blocking collectives, local(): fitted_raw, norm_snp = lax.psum((fitted_part, norm_part), 'snp')  49.9 us
    psum x1, waiting for transfers between devices, local(): fitted_raw, norm_snp = lax.psum((fitted_part, norm_part), 'snp')  37.2 us
  transfers between devices with their start and end apart: 3, of which 3 were waited for; matrix products, arithmetic and copies ran while one was open for 0% of the time, Pallas kernels for 0%

commit v1 on v0

v1 whole, which is shorter than its diff:
```python
import functools

import jax
import jax.numpy as jnp
from jax import lax
from jax.experimental import pallas as pl
from jax.experimental.pallas import tpu as pltpu
from jax.sharding import PartitionSpec as P

MESH = pl.DeviceIdType.MESH
F32, BF16 = jnp.float32, jnp.bfloat16
HIGHEST = lax.Precision.HIGHEST
SIZE = {"x": 4, "y": 2, "z": 8}
ROWS, SNPS, TRAITS, RANK = 512, 4096, 256, 64
SAMPLES = 64 * ROWS
PARTS = ((("x", "z", "y"), 0, 32), (("y", "x", "z"), 2048, 32))


def rows_of(part):
    return part[2] * 64


def kernel(g_hbm, t_hbm, basis_ref, fit_ref, cov_ref, score_ref, *scratch):
    it = iter(scratch)
    g, t, raw, gsum = next(it), next(it), next(it), next(it)
    tsum, tsum_in, tile, tile_in, mean_all, norm_in = (next(it) for _ in range(6))
    parts = [tuple(next(it) for _ in range(8)) for _ in PARTS]
    p, pb, pb_in, half, hb, hb_in, full = (next(it) for _ in range(7))
    gt, gt_in, gz_in, gx_in, gy_in, gall = (next(it) for _ in range(6))
    load_sem, send_sem, recv_sem = next(it), next(it), next(it)

    samp, snp = lax.axis_index("samp"), lax.axis_index("snp")
    me = {"x": lax.rem(samp // 2, 4), "y": lax.rem(samp, 2), "z": samp // 8}
    yh, core = snp // 2, lax.rem(snp, 2)

    def at(dim, k):
        n = SIZE[dim]
        to = lax.rem(me[dim] + k, n)
        c = dict(me)
        c[dim] = to
        return to, ((c["z"] * 4 + c["x"]) * 2 + c["y"], snp)

    other_core = (samp, yh * 2 + (1 - core))
    other_half = (samp, (1 - yh) * 2 + core)
    y_peer = at("y", 1)[1]
    y_far = (y_peer[0], other_half[1])

    peers = [at(d, k)[1] for d in "xyz" for k in range(1, SIZE[d])]
    peers += [other_core, other_half, y_far]
    barrier = pltpu.get_barrier_semaphore()
    for dev in peers:
        pl.semaphore_signal(barrier, inc=1, device_id=dev, device_id_type=MESH)

    t_copy = pltpu.make_async_copy(t_hbm, t, load_sem.at[4])
    t_copy.start()
    g_copies = []
    for i in range(4):
        cols = pl.ds(i * 1024, 1024)
        cp = pltpu.make_async_copy(g_hbm.at[:, cols], g.at[:, cols], load_sem.at[i])
        cp.start()
        g_copies.append(cp)

    count = [0]
    started = []

    def send(src, dst, dev):
        i = count[0]
        count[0] += 1
        cp = pltpu.make_async_remote_copy(
            src_ref=src, dst_ref=dst, send_sem=send_sem.at[i], recv_sem=recv_sem.at[i],
            device_id=dev, device_id_type=MESH)
        cp.start()
        started.append(cp)
        return cp

    def wait(copies):
        for cp in copies:
            cp.wait_recv()

    t_copy.wait()

    def add_rows(i, acc):
        b = t[pl.ds(pl.multiple_of(i * 64, 64), 64), :].astype(F32)
        return acc + jnp.sum(b.reshape(8, 8, TRAITS), axis=0)

    acc = lax.fori_loop(0, ROWS // 64, add_rows, jnp.zeros((8, TRAITS), F32))
    tot = jnp.sum(acc, axis=0, keepdims=True)
    tsum[0] = jnp.concatenate([tot] * 8, axis=0)
    pl.semaphore_wait(barrier, len(peers))

    ones = jnp.ones((ROWS, 128), BF16)

    def product(i):
        cols = pl.ds(i * 512, 512)
        blk = g[:, cols]
        dims = (((0,), (0,)), ((), ()))
        raw[cols, :] = lax.dot_general(blk, t[...], dims, preferred_element_type=F32)
        gsum[cols, :] = lax.dot_general(blk, ones, dims, preferred_element_type=F32)

    slot = 0
    blocks = [[0, 1, 2], [3, 4, 5], [6, 7]]
    for s, d in enumerate("xzy"):
        n = SIZE[d]
        cps = [send(tsum.at[s], tsum_in.at[slot + k - 1], at(d, k)[1]) for k in range(1, n)]
        for i in blocks[s]:
            if i % 2 == 0:
                g_copies[i // 2].wait()
            product(i)
        wait(cps)
        v = tsum[s]
        for k in range(n - 1):
            v = v + tsum_in[slot + k]
        tsum[s + 1] = v
        slot += n - 1

    def centred(r0, n):
        rows = pl.ds(r0, n)
        c = tsum[3] * (1.0 / SAMPLES)
        c = jnp.concatenate([c] * (n // 8), axis=0)
        s = gsum[rows, :]
        return raw[rows, :] - jnp.concatenate([s, s], axis=1) * c

    def stage_one(part, bufs):
        order, first, own = part
        d = order[0]
        n = SIZE[d]
        blk = rows_of(part) // n
        out, inn = bufs[0], bufs[1]
        cps = []
        for k in range(1, n):
            to, dev = at(d, k)

            def fill(i, _):
                r = pl.multiple_of(i * 32, 32)
                out[k - 1, pl.ds(r, 32), :] = centred(pl.multiple_of(first + to * blk + r, 32), 32).astype(BF16)
                return 0

            lax.fori_loop(0, blk // 32, fill, 0)
            cps.append(send(out.at[k - 1], inn.at[k - 1], dev))
        return cps

    def sum_one(part, bufs):
        order, first, own = part
        n = SIZE[order[0]]
        blk = rows_of(part) // n
        inn, two = bufs[1], bufs[2]
        mine = me[order[0]]
        sub = blk // SIZE[order[1]]

        def body(i, _):
            r = pl.multiple_of(i * 32, 32)
            v = centred(pl.multiple_of(first + mine * blk + r, 32), 32)
            for k in range(n - 1):
                v = v + inn[k, pl.ds(r, 32), :].astype(F32)
            two[pl.ds(r, 32), :] = v.astype(BF16)

            @pl.when(r // sub == me[order[1]])
            def _():
                bufs[7][pl.ds(pl.multiple_of(lax.rem(r, sub), 32), 32), :] = v
            return 0

        lax.fori_loop(0, blk // 32, body, 0)

    def stage_two(part, bufs):
        order, first, own = part
        d = order[1]
        sub = own * SIZE[order[2]]
        cps = []
        for k in range(1, SIZE[d]):
            to, dev = at(d, k)
            cps.append(send(bufs[2].at[pl.ds(pl.multiple_of(to * sub, 32), sub), :], bufs[3].at[k - 1], dev))
        return cps

    def sum_two(part, bufs):
        order, first, own = part
        n = SIZE[order[1]]
        sub = own * SIZE[order[2]]

        def body(i, _):
            r = pl.multiple_of(i * 32, 32)
            v = bufs[7][pl.ds(r, 32), :]
            for k in range(n - 1):
                v = v + bufs[3][k, pl.ds(r, 32), :].astype(F32)
            bufs[7][pl.ds(r, 32), :] = v
            bufs[4][pl.ds(r, 32), :] = v.astype(BF16)
            return 0

        lax.fori_loop(0, sub // 32, body, 0)

    def stage_three(part, bufs):
        order, first, own = part
        d = order[2]
        cps = []
        for k in range(1, SIZE[d]):
            to, dev = at(d, k)
            cps.append(send(bufs[4].at[pl.ds(pl.multiple_of(to * own, 16), own), :], bufs[5].at[k - 1], dev))
        return cps

    def where(part):
        order = part[0]
        return tuple(me[d] for d in order)

    def sum_three(part, bufs):
        order, first, own = part
        n = SIZE[order[2]]
        v = bufs[7][pl.ds(pl.multiple_of(me[order[2]] * own, 16), own), :]
        for k in range(n - 1):
            v = v + bufs[5][k].astype(F32)
        a, b, c = where(part)
        bufs[6][a, b, c] = v.astype(BF16)
        return jnp.sum(v * v, axis=0, keepdims=True)

    both = list(zip(PARTS, parts))
    one = [stage_one(*pb_) for pb_ in both]
    two, three = [], []
    for pb_, cps in zip(both, one):
        wait(cps)
        sum_one(*pb_)
        two.append(stage_two(*pb_))
    for pb_, cps in zip(both, two):
        wait(cps)
        sum_two(*pb_)
        three.append(stage_three(*pb_))
    norm = jnp.zeros((1, TRAITS), F32)
    gather = []
    for (part, bufs), cps in zip(both, three):
        wait(cps)
        norm = norm + sum_three(part, bufs)
        a, b, c = where(part)
        piece = bufs[6].at[a, b, c]
        gather.append([send(piece, piece, at(part[0][2], k)[1]) for k in range(1, SIZE[part[0][2]])])
    norm8 = jnp.concatenate([norm[:, :128], norm[:, 128:]] + [jnp.zeros((6, 128), F32)], axis=0)
    tile[0] = norm8

    def norm_step(s, d, slot):
        n = SIZE[d]
        return [send(tile.at[s], norm_in.at[slot + k - 1], at(d, k)[1]) for k in range(1, n)]

    def norm_sum(s, d, slot):
        v = tile[s]
        for k in range(SIZE[d] - 1):
            v = v + norm_in[slot + k]
        tile[s + 1] = v

    nx = norm_step(0, "x", 0)
    gather2 = []
    for (part, bufs), cps in zip(both, gather):
        wait(cps)
        a, b, c = where(part)
        piece = bufs[6].at[a, b]
        gather2.append([send(piece, piece, at(part[0][1], k)[1]) for k in range(1, SIZE[part[0][1]])])
    wait(nx)
    norm_sum(0, "x", 0)
    nz = norm_step(1, "z", 3)
    gather3 = []
    for (part, bufs), cps in zip(both, gather2):
        wait(cps)
        a, b, c = where(part)
        piece = bufs[6].at[a]
        gather3.append([send(piece, piece, at(part[0][0], k)[1]) for k in range(1, SIZE[part[0][0]])])
    wait(nz)
    norm_sum(1, "z", 3)
    ny = norm_step(2, "y", 10)

    def project(part, bufs, a, start):
        order, first, own = part
        blk = rows_of(part) // SIZE[order[0]]
        cols = pl.ds(pl.multiple_of(first + a * blk, 128), blk)
        v = jnp.dot(g[:, cols], bufs[6][a].reshape(blk, TRAITS), preferred_element_type=F32)
        if start:
            p[...] = v
        else:
            p[...] += v

    for i, (part, bufs) in enumerate(both):
        project(part, bufs, me[part[0][0]], i == 0)
    wait(ny)
    norm_sum(2, "y", 10)
    for (part, bufs), cps in zip(both, gather3):
        d = part[0][0]
        for k, cp in enumerate(cps):
            cp.wait_recv()
            project(part, bufs, lax.rem(me[d] + SIZE[d] - (k + 1), SIZE[d]), False)

    mean = jnp.sum(p[...], axis=0, keepdims=True) * (1.0 / ROWS)
    tile[4] = jnp.concatenate([mean[:, :128], mean[:, 128:], tile[3][:2], jnp.zeros((4, 128), F32)], axis=0)
    away = pl.multiple_of((1 - core) * 256, 256)
    pb[...] = p[pl.ds(away, 256), :] - mean
    c1 = [send(pb, pb_in, other_core), send(tile.at[4], tile_in.at[0], other_core)]
    wait(c1)
    tile[5] = tile[4] + tile_in[0]
    half[...] = p[pl.ds(pl.multiple_of(core * 256, 256), 256), :] - mean + pb_in[...]
    hb[...] = half[pl.ds(pl.multiple_of((1 - yh) * 128, 128), 128), :]
    c2 = [send(hb, hb_in, other_half), send(tile.at[5], tile_in.at[1], other_half)]
    wait(c2)
    tile[6] = tile[5] + tile_in[1]
    mine = half[pl.ds(pl.multiple_of(yh * 128, 128), 128), :] + hb_in[...]
    full[core, yh] = mine
    c3 = [send(full.at[core, yh], full.at[core, yh], other_half)]

    mean_all[me["z"], me["x"], me["y"]] = tile[6]
    piece = mean_all.at[me["z"], me["x"], me["y"]]
    m1 = [send(piece, piece, at("x", k)[1]) for k in range(1, 4)]

    dims0 = (((0,), (0,)), ((), ()))
    a_gram = lax.dot_general(mine, mine, dims0, precision=HIGHEST, preferred_element_type=F32)
    for r in range(32):
        for c in range(2):
            gt[r // 16, (r // 2) % 8, (r % 2) * 2 + c] = a_gram[r * 8:r * 8 + 8, c * 128:c * 128 + 128]
    g1 = [send(gt.at[1 - core], gt_in, other_core)]
    wait(g1)
    for z in range(8):
        gt_in[z] = gt_in[z] + gt[core, z]
    g2 = []
    for k in range(1, 8):
        to, dev = at("z", k)
        g2.append(send(gt_in.at[to], gz_in.at[k - 1], dev))
    wait(m1)
    piece = mean_all.at[me["z"], :, me["y"]]
    m2 = []
    for x in range(4):
        piece = mean_all.at[me["z"], x, me["y"]]
        m2 += [send(piece, piece, at("z", k)[1]) for k in range(1, 8)]
    wait(g2)
    v = gt_in[me["z"]]
    for k in range(7):
        v = v + gz_in[k]
    gz_in[7] = v
    g3 = []
    for k in range(1, 4):
        to, dev = at("x", k)
        g3.append(send(gz_in.at[7, to], gx_in.at[k - 1], dev))
    wait(c3)
    c4 = [send(full.at[core], full.at[core], other_core)]
    wait(g3)
    v = gz_in[7, me["x"]]
    for k in range(3):
        v = v + gx_in[k]
    gy_in[3] = v
    g4 = [send(gy_in.at[3], gy_in.at[i], dev) for i, dev in enumerate((y_peer, other_half, y_far))]
    wait(g4)
    gall[core, me["z"], me["x"]] = gy_in[3] + gy_in[0] + (gy_in[1] + gy_in[2])
    piece = gall.at[core, me["z"], me["x"]]
    g5 = [send(piece, piece, at("x", k)[1]) for k in range(1, 4)]
    wait(m2)
    m3 = []
    for z in range(8):
        for x in range(4):
            piece = mean_all.at[z, x, me["y"]]
            m3.append(send(piece, piece, y_peer))
    wait(g5)
    piece = gall.at[core, me["z"]]
    g6 = [send(piece, piece, at("z", k)[1]) for k in range(1, 8)]
    wait(g6)
    piece = gall.at[core]
    g7 = [send(piece, piece, other_core)]
    wait(m3)
    wait(c4)
    means = jnp.concatenate([mean_all[z, x, y] for z in range(8) for x in range(4) for y in range(2)], axis=0)
    means = means.reshape(64, 8, 128)
    means = jnp.concatenate([means[:, 0, :], means[:, 1, :]], axis=1)
    centre = jnp.sum(means, axis=0, keepdims=True) * (1.0 / 64)
    dev_ = means - centre
    between = lax.dot_general(dev_, dev_, dims0, precision=HIGHEST, preferred_element_type=F32) * float(ROWS)
    norm_row = jnp.concatenate([tile[6][2:3], tile[6][3:4]], axis=1)
    off = jnp.concatenate([tile[6][0:1], tile[6][1:2]], axis=1) - centre
    wait(g7)
    rows = []
    for r in range(32):
        rows.append(jnp.concatenate(
            [gall[r // 16, (r // 2) % 8, (r % 2) * 2 + c] for c in range(2)], axis=1))
    gram = jnp.concatenate(rows, axis=0) + between
    eye = (lax.broadcasted_iota(jnp.int32, (TRAITS, TRAITS), 0)
           == lax.broadcasted_iota(jnp.int32, (TRAITS, TRAITS), 1))
    diag = jnp.where(eye, gram, 0.0)
    diag_row = jnp.sum(diag, axis=0, keepdims=True)
    step_row = norm_row / (diag_row + (SAMPLES / 8.0) * norm_row)
    step_col = jnp.sum(jnp.where(eye, jnp.broadcast_to(step_row, (TRAITS, TRAITS)), 0.0), axis=1, keepdims=True)
    cov = step_col * gram * step_row * (1.0 / SAMPLES)
    cov_ref[...] = cov
    spread = jnp.sum(step_row * step_row * diag_row, axis=1, keepdims=True) * (1.0 / SAMPLES) + 1e-6
    loading = jnp.dot(cov, basis_ref[...], precision=HIGHEST, preferred_element_type=F32) * (TRAITS / spread)
    high = loading.astype(BF16)
    low = (loading - high.astype(F32)).astype(BF16)
    for c in range(2):
        for h in range(2):
            r = pl.ds((c * 2 + h) * 128, 128)
            f = ((full[c, h] + off) * step_row).astype(BF16)
            fit_ref[r, :] = f
            score_ref[r, :] = (jnp.dot(f, high, preferred_element_type=F32)
                               + jnp.dot(f, low, preferred_element_type=F32))
    for cp in started:
        cp.wait_send()
    assert count[0] == COPIES, count[0]


COPIES = 160


def scratch_of():
    vmem = pltpu.VMEM
    shapes = [
        vmem((ROWS, SNPS), BF16), vmem((ROWS, TRAITS), BF16), vmem((SNPS, TRAITS), F32), vmem((SNPS, 128), F32),
        vmem((4, 8, TRAITS), F32), vmem((11, 8, TRAITS), F32),
        vmem((7, 8, 128), F32), vmem((2, 8, 128), F32), vmem((8, 4, 2, 8, 128), F32), vmem((11, 8, 128), F32),
    ]
    for part in PARTS:
        order, first, own = part
        n1, n2, n3 = (SIZE[d] for d in order)
        rows = rows_of(part)
        shapes += [
            vmem((n1 - 1, rows // n1, TRAITS), BF16), vmem((n1 - 1, rows // n1, TRAITS), BF16),
            vmem((rows // n1, TRAITS), BF16), vmem((n2 - 1, own * n3, TRAITS), BF16),
            vmem((own * n3, TRAITS), BF16), vmem((n3 - 1, own, TRAITS), BF16),
            vmem((n1, n2, n3, own, TRAITS), BF16), vmem((own * n3, TRAITS), F32),
        ]
    shapes += [
        vmem((ROWS, TRAITS), F32), vmem((256, TRAITS), F32), vmem((256, TRAITS), F32), vmem((256, TRAITS), F32),
        vmem((128, TRAITS), F32), vmem((128, TRAITS), F32), vmem((2, 2, 128, TRAITS), F32),
        vmem((2, 8, 4, 8, 128), F32), vmem((8, 4, 8, 128), F32), vmem((8, 4, 8, 128), F32), vmem((3, 8, 128), F32),
        vmem((4, 8, 128), F32), vmem((2, 8, 4, 8, 128), F32),
        pltpu.SemaphoreType.DMA((5,)), pltpu.SemaphoreType.DMA((COPIES,)), pltpu.SemaphoreType.DMA((COPIES,)),
    ]
    return shapes


def local(genotypes, traits, trait_basis):
    anywhere = pl.BlockSpec(memory_space=pl.ANY)
    inside = pl.BlockSpec(memory_space=pltpu.VMEM)
    return pl.pallas_call(
        kernel,
        out_shape=(
            jax.ShapeDtypeStruct((ROWS, TRAITS), BF16),
            jax.ShapeDtypeStruct((TRAITS, TRAITS), F32),
            jax.ShapeDtypeStruct((ROWS, RANK), F32),
        ),
        in_specs=[anywhere, anywhere, inside],
        out_specs=(inside, inside, inside),
        scratch_shapes=scratch_of(),
        compiler_params=pltpu.CompilerParams(
            collective_id=0, has_side_effects=True, vmem_limit_bytes=56 * 2**20),
    )(genotypes, traits, trait_basis)


def solution(mesh):
    return jax.shard_map(
        local,
        mesh=mesh,
        in_specs=(P("samp", "snp"), P("samp", None), P()),
        out_specs=(P("samp", None), P(), P("samp", None)),
        check_vma=False,
    )
```

time: 1560 us -> 118 us (0.08); the launches traced: 1530 us -> 118 us
  waiting for transfers between devices: 1050 us -> 0 us
  blocking collectives: 439 us -> 0 us
  Pallas kernels: 0 us -> 111 us
  matrix products: 17.4 us -> 0 us
    psum x3 -> x0, waiting for transfers between devices: 1050 us -> none  [the longest x1 627 us: local(): lax.psum(product - geno_mean[:, None] * trait_local[None, :], 'samp')]
    psum x3 -> x0, blocking collectives: 439 us -> none  [the longest x1 257 us: local(): lax.psum(jnp.sum(genotypes, axis=0, dtype=jnp.float32), 'samp')]
    pallas_call x0 -> x1, Pallas kernels: none -> 111 us  [local(): pl.pallas_call(kernel, out_shape=(jax.ShapeDtypeStruct((ROWS, TRAITS), BF...]
    dot_general x6 -> x0, matrix products: 17.4 us -> none  [the longest x1 5.9 us: local(): lax.dot_general(genotypes, traits, (((0,), (0,)), ((), ())), preferred_el...]
  transfers between devices with their start and end apart: 3 -> 0, of which waited for: 3 -> 0; matrix products, arithmetic and copies ran while one was open for 0% -> 0% of each run, Pallas kernels for 0% -> 0%
where the time goes in v1:
time: 118 us
  Pallas kernels  111 us (94%)
  local copies, waits for them, and re-layouts  6.65 us (6%)
    pallas_call x1, Pallas kernels, local(): pl.pallas_call(kernel, out_shape=(jax.ShapeDtypeStruct((ROWS, TRAITS), BF...  111 us
    unnamed x3, local copies, waits for them, and re-layouts  4.93 us

profile of v1, /device:TPU:1, one launch (start us, length us, event | category | flops | bytes accessed | tf_op | source)
XLA Modules:
  0.0 117.8 jit_solution(10165285618444279471)
XLA Ops:
  0.6 1.6 %copy.6.basis_ref = f32[256,64]{1,0:T(8,128)} copy(f32[256,64]{0,1:T(8,128)} %param.5) | data formatting | bytes 131072 | tf_op args[2]
  2.2 110.5 %shard_map.58 = (bf16[512,256]{1,0:T(8,128)(2,1)}, f32[256,256]{1,0:T(8,128)}, f32[512,64]{1,0:T(8,128)}) custom-call(bf16[512,4096]{1,0:T(8,128)(2,1)} %g_hbm.1, bf16[512,256]{1,0:T(8,128)(2,1)} %t_hbm.1, f32[256,64]{1,0:T(8,128)} %copy.6.basis_ref), custom_call_target="tpu_custom_call" | custom-call | tf_op jit(solution)/shard_map/pallas_call | solution.py:430
  112.8 1.7 %copy.7 = f32[512,64]{0,1:T(8,128)} copy(f32[512,64]{1,0:T(8,128)} %get-tuple-element.5) | data formatting | bytes 262144 | tf_op jit(solution)/shard_map/pallas_call | solution.py:430
  114.5 1.7 %copy.10 = bf16[512,256]{1,0:T(8,128)(2,1)} copy(bf16[512,256]{1,0:T(8,128)(2,1)} %get-tuple-element.9) | data formatting | bytes 524288
  116.2 1.7 %copy.11 = f32[256,256]{1,0:T(8,128)} copy(f32[256,256]{1,0:T(8,128)} %get-tuple-element.10) | data formatting | bytes 524288

commit v2 on v0

v2 whole, which is shorter than its diff:
```python
import itertools

import jax
import jax.numpy as jnp
from jax import lax
from jax.experimental import pallas as pl
from jax.experimental.pallas import tpu as pltpu
from jax.sharding import PartitionSpec as P

MESH = pl.DeviceIdType.MESH
F32, BF16 = jnp.float32, jnp.bfloat16
HIGHEST = lax.Precision.HIGHEST
SIZE = {"x": 4, "y": 2, "z": 8, "h": 2}
ROWS, SNPS, TRAITS, RANK = 512, 4096, 256, 64
GROUPS = 64
SAMPLES = GROUPS * ROWS
DIMS0 = (((0,), (0,)), ((), ()))
PLANE, ALONG = ("x", "y"), ("z",)
PARTS = ((PLANE, ALONG), (ALONG, PLANE), (PLANE, ALONG), (PLANE, ALONG))
PART = SNPS // len(PARTS)
OWN = PART // GROUPS
ORDER = [(0, 0), (1, 0), (2, 0), (3, 0), (0, 1), (2, 1), (1, 1), (0, 2), (3, 1), (2, 2), (1, 2), (0, 3), (3, 2), (2, 3),
         (1, 3), (3, 3), (0, 4), (2, 4), (1, 4), (3, 4)]


SLOTS = {PLANE: (0, 1, 2, 3, 4, 5, 6), ("x",): (1, 3, 5), ("y",): (0,)}


def size_of(group):
    n = 1
    for d in group:
        n *= SIZE[d]
    return n


def steps_of(part):
    return 2 * len(part) + 1


def order_of():
    if ORDER is not None:
        return ORDER
    first = [(i, 0) for i in range(len(PARTS))]
    return first + [(i, t - i) for t in range(16) for i in range(len(PARTS)) if 0 < t - i < steps_of(PARTS[i])]


def dot_rows(a, b):
    return lax.dot_general(a, b, DIMS0, precision=HIGHEST, preferred_element_type=F32)


def kernel(g_hbm, t_hbm, gram_ref, stat_ref, proj_hbm, *scratch):
    it = iter(scratch)
    g, t, raw, gsum = (next(it) for _ in range(4))
    mean, mean_in = {}, {}
    for grp in (PLANE, ALONG):
        mean[grp], mean_in[grp] = next(it), next(it)
    wide, wide_in = next(it), next(it)
    bufs = []
    for part in PARTS:
        b = {"s_out": next(it), "s_in": next(it), "out": next(it), "corr": next(it)}
        b["in"] = [next(it) for _ in part]
        b["acc"] = [None] + [next(it) for _ in part[1:]]
        b["low"] = [None] + [next(it) for _ in part[1:]]
        b["n"] = next(it)
        bufs.append(b)
    p, pb, pb_in, half, hb, hb_in, full = (next(it) for _ in range(7))
    tile, tile_in, every = next(it), next(it), next(it)
    gt, gc_in, gz_in, gh, gh_in, gall = (next(it) for _ in range(6))
    load_sem, send_sem, recv_sem = next(it), next(it), next(it)

    samp, snp = lax.axis_index("samp"), lax.axis_index("snp")
    me = {"x": lax.rem(samp // 2, 4), "y": lax.rem(samp, 2), "z": samp // 8, "h": snp // 2}
    core = lax.rem(snp, 2)

    def index(group, c=me):
        i = 0
        for d in group:
            i = i * SIZE[d] + c[d]
        return i

    def peers(group):
        for ks in itertools.product(*(range(SIZE[d]) for d in group)):
            if any(ks):
                c = dict(me)
                for d, k in zip(group, ks):
                    c[d] = lax.rem(me[d] + k, SIZE[d])
                yield index(group, c), ((c["z"] * 4 + c["x"]) * 2 + c["y"], c["h"] * 2 + core)

    plane, along = list(peers(PLANE)), list(peers(ALONG))
    layer = list(peers(("x", "y", "h")))
    (_, other_half), = peers(("h",))
    other_core = (samp, me["h"] * 2 + (1 - core))
    met = [dev for _, dev in layer + along] + [other_core]

    barrier = pltpu.get_barrier_semaphore()
    for dev in met:
        pl.semaphore_signal(barrier, inc=1, device_id=dev, device_id_type=MESH)
    t_copy = pltpu.make_async_copy(t_hbm, t, load_sem.at[0])
    t_copy.start()
    g_copies = []
    for i in range(len(PARTS)):
        cols = pl.ds(i * PART, PART)
        cp = pltpu.make_async_copy(g_hbm.at[:, cols], g.at[:, cols], load_sem.at[1 + i])
        cp.start()
        g_copies.append(cp)

    count = [0]
    started = []

    def send(src, dst, dev):
        i = count[0]
        count[0] += 1
        cp = pltpu.make_async_remote_copy(
            src_ref=src, dst_ref=dst, send_sem=send_sem.at[i], recv_sem=recv_sem.at[i],
            device_id=dev, device_id_type=MESH)
        cp.start()
        started.append(cp)
        return cp

    def wait(copies):
        for cp in copies:
            cp.wait_recv()

    t_copy.wait()

    def add_rows(i, acc):
        b = t[pl.ds(pl.multiple_of(i * 64, 64), 64), :].astype(F32)
        return acc + jnp.sum(b.reshape(8, 8, TRAITS), axis=0)

    acc = lax.fori_loop(0, ROWS // 64, add_rows, jnp.zeros((8, TRAITS), F32))
    own_mean = jnp.broadcast_to(jnp.sum(acc, axis=0, keepdims=True) * (1.0 / ROWS), (8, TRAITS))
    for grp in (PLANE, ALONG):
        mean[grp][...] = own_mean
    pl.semaphore_wait(barrier, len(met))
    c_plane = [send(mean[PLANE], mean_in[PLANE].at[k], dev) for k, (_, dev) in enumerate(plane)]
    c_along = [] if all(part[0] != ALONG for part in PARTS) else [send(mean[ALONG], mean_in[ALONG].at[k], dev) for k, (_, dev) in enumerate(along)]

    ones_col = jnp.ones((ROWS, 128), BF16)
    ones_row = jnp.ones((8, ROWS), BF16)
    sent = [dict() for _ in PARTS]
    norms = []

    def devices(part, s):
        return {PLANE: plane, ALONG: along}[part[s]] if part[s] in (PLANE, ALONG) else list(peers(part[s]))

    def blocks(part):
        out, n = [], PART
        for grp in part:
            n //= size_of(grp)
            out.append(n)
        return out

    def centred(r, n):
        c = jnp.concatenate([mean[PLANE][...]] * (n // 8), axis=0)
        s = gsum[pl.ds(r, n), :]
        return raw[pl.ds(r, n), :] - jnp.concatenate([s, s], axis=1) * c

    def first_send(i):
        part, b = PARTS[i], bufs[i]
        blk = blocks(part)[0]
        g_copies[i].wait()
        for j in range(PART // 512):
            cols = pl.ds(i * PART + j * 512, 512)
            piece = g[:, cols]
            raw[cols, :] = lax.dot_general(piece, t[...], DIMS0, preferred_element_type=F32)
            gsum[cols, :] = lax.dot_general(piece, ones_col, DIMS0, preferred_element_type=F32)
            sums = jnp.dot(ones_row, piece, preferred_element_type=F32)[:1]
            for q in range(4):
                lane = j * 512 + q * 128
                b["s_out"][lane // blk, pl.ds((lane % blk) // 128, 1), :] = sums[:, q * 128:q * 128 + 128]
        s_cp = []
        for k, (to, dev) in enumerate(devices(part, 0)):
            s_cp.append(send(b["s_out"].at[to], b["s_in"].at[k], dev))
        cps = []
        for k, (to, dev) in enumerate(devices(part, 0)):
            def fill(j, _):
                r = pl.multiple_of(j * 64, 64)
                b["out"][k, pl.ds(r, 64), :] = centred(pl.multiple_of(i * PART + to * blk + r, 64), 64).astype(BF16)
                return 0
            lax.fori_loop(0, blk // 64, fill, 0)
            cps.append(send(b["out"].at[k], b["in"][0].at[k], dev))
        sent[i]["s"], sent[i]["rs"] = s_cp, cps

    def reduce(i, s):
        part, b = PARTS[i], bufs[i]
        blk = blocks(part)[s]
        n = size_of(part[s])
        last = s == len(part) - 1
        mine = index(part[s])
        if s == 0:
            wait(sent[i]["s"])
            grp = part[0]
            if grp == ALONG:
                wait(c_along)
                c_along.clear()
            means, slots = (ALONG, range(7)) if grp == ALONG else (PLANE, SLOTS[grp])
            width = blk // 128
            lines = [b["s_out"].at[mine]] + [b["s_in"].at[k] for k in range(n - 1)]
            sums = jnp.concatenate(
                [jnp.concatenate([ref[pl.ds(q, 1), :] for q in range(width)], axis=1) for ref in lines]
                + [jnp.zeros((8 - n, blk), F32)] * (n < 8), axis=0)
            gaps = jnp.concatenate(
                [mean[means][:1]] + [mean_in[means][k, :1] for k in slots]
                + [jnp.zeros((8 - n, TRAITS), F32)] * (n < 8), axis=0) - wide[1, :1]
            b["corr"][...] = dot_rows(sums, gaps)
        wait(sent[i]["rs"])
        rows = min(blk, 64)

        def body(j, norm):
            r = pl.multiple_of(j * rows, rows)
            if s == 0:
                v = centred(pl.multiple_of(i * PART + mine * blk + r, rows), rows) + b["corr"][pl.ds(r, rows), :]
            else:
                v = b["acc"][s][pl.ds(pl.multiple_of(mine * blk + r, rows), rows), :]
            for k in range(n - 1):
                v = v + b["in"][s][k, pl.ds(r, rows), :].astype(F32)
            if last:
                b["n"][tuple(index(grp) for grp in part)] = v.astype(BF16)
                return norm + jnp.sum(v * v, axis=0, keepdims=True)
            b["acc"][s + 1][pl.ds(r, rows), :] = v
            b["low"][s + 1][pl.ds(r, rows), :] = v.astype(BF16)
            return norm

        norm = lax.fori_loop(0, blk // rows, body, jnp.zeros((1, TRAITS), F32))
        if last:
            norms.append(norm)
            gather(i, s)
            return
        nxt = blocks(part)[s + 1]
        sent[i]["rs"] = [
            send(b["low"][s + 1].at[pl.ds(pl.multiple_of(to * nxt, nxt), nxt), :], b["in"][s + 1].at[k], dev)
            for k, (to, dev) in enumerate(devices(part, s + 1))]

    def gather(i, s):
        part, b = PARTS[i], bufs[i]
        piece = b["n"].at[tuple(index(grp) for grp in part[:s + 1])]
        sent[i]["ag"] = [send(piece, piece, dev) for _, dev in devices(part, s)]

    def project(i):
        v = jnp.dot(g[:, pl.ds(i * PART, PART)], bufs[i]["n"][...].reshape(PART, TRAITS), preferred_element_type=F32)
        if not projected:
            p[...] = v
        else:
            p[...] += v
        projected.append(i)

    projected = []
    for turn, (i, step) in enumerate(order_of()):
        stages = len(PARTS[i])
        if step == 0:
            first_send(i)
        elif step <= stages:
            if turn and wide_send:
                wait(wide_send)
                v = wide[0]
                for k in range(7):
                    v = v + wide_in[k]
                wide[1] = v * (1.0 / GROUPS)
                wide_send.clear()
            reduce(i, step - 1)
        else:
            wait(sent[i]["ag"])
            s = 2 * stages - step - 1
            if s >= 0:
                gather(i, s)
            else:
                project(i)
        if turn == 0:
            wait(c_plane)
            v = mean[PLANE][...]
            for k in range(7):
                v = v + mean_in[PLANE][k]
            wide[0] = v
            wide_send = [send(wide.at[0], wide_in.at[k], dev) for k, (_, dev) in enumerate(along)]

    norm = norms[0]
    for v in norms[1:]:
        norm = norm + v
    own = jnp.sum(p[...], axis=0, keepdims=True) * (1.0 / ROWS)
    tile[0] = jnp.concatenate([own[:, :128], own[:, 128:], norm[:, :128], norm[:, 128:], jnp.zeros((4, 128), F32)], axis=0)
    pb[...] = p[pl.ds(pl.multiple_of((1 - core) * 256, 256), 256), :] - own
    c1 = [send(pb, pb_in, other_core), send(tile.at[0], tile_in.at[0], other_core)]
    wait(c1)
    tile[1] = tile[0] + tile_in[0]
    half[...] = p[pl.ds(pl.multiple_of(core * 256, 256), 256), :] - own + pb_in[...]
    hb[...] = half[pl.ds(pl.multiple_of((1 - me["h"]) * 128, 128), 128), :]
    c2 = [send(hb, hb_in, other_half), send(tile.at[1], tile_in.at[1], other_half)]
    wait(c2)
    tile[2] = tile[1] + tile_in[1]
    mine = half[pl.ds(pl.multiple_of(me["h"] * 128, 128), 128), :] + hb_in[...]
    full[core, me["h"]] = mine

    a_gram = lax.dot_general(mine, mine, DIMS0, precision=HIGHEST, preferred_element_type=F32)
    gt[...] = a_gram.reshape(2, 8, 16, TRAITS)
    g1 = [send(gt.at[1 - core], gc_in, other_core)]
    c3 = [send(full.at[core, me["h"]], full.at[core, me["h"]], other_half)]
    spot = index(PLANE)
    every[spot, me["z"]] = tile[2]
    m1 = [send(every.at[spot, me["z"]], every.at[spot, me["z"]], dev) for _, dev in along]
    wait(g1)
    gc_in[...] = gc_in[...] + gt[core]
    g2 = [send(gc_in.at[to], gz_in.at[k], dev) for k, (to, dev) in enumerate(along)]
    wait(g2)
    v = gc_in[me["z"]]
    for k in range(7):
        v = v + gz_in[k]
    gh[...] = v
    g3 = [send(gh, gh_in.at[k], dev) for k, (_, dev) in enumerate(layer)]
    wait(m1)
    m2 = [send(every.at[spot], every.at[spot], dev) for _, dev in plane]
    wait(c3)
    c4 = [send(full.at[core], full.at[core], other_core)]
    wait(g3)
    v = gh[...]
    for k in range(15):
        v = v + gh_in[k]
    gall[core, me["z"]] = v
    piece = gall.at[core, me["z"]]
    g4 = [send(piece, piece, dev) for _, dev in along]
    wait(c4)
    proj_copy = pltpu.make_async_copy(full, proj_hbm, load_sem.at[0])
    proj_copy.start()
    wait(g4)
    g5 = [send(gall.at[core], gall.at[core], other_core)]
    wait(m2)
    means = jnp.concatenate([every[:, :, r, :].reshape(GROUPS, 128) for r in range(2)], axis=1)
    norm = jnp.concatenate(
        [jnp.sum(every[:, :, r, :].reshape(GROUPS, 128), axis=0, keepdims=True) for r in (2, 3)], axis=1)
    centre = jnp.sum(means, axis=0, keepdims=True) * (1.0 / GROUPS)
    gap = means - centre
    between = dot_rows(gap, gap) * float(ROWS)
    off = jnp.concatenate([tile[2, 0:1], tile[2, 1:2]], axis=1) - centre
    stat_ref[...] = jnp.concatenate([norm, off, jnp.zeros((6, TRAITS), F32)], axis=0)
    wait(g5)
    gram_ref[...] = gall[...].reshape(TRAITS, TRAITS) + between
    for cp in started:
        cp.wait_send()
    proj_copy.wait()
    assert count[0] == COPIES, count[0]


COPIES = 65 + 7 * any(part[0] == ALONG for part in PARTS) + sum(
    size_of(part[0]) - 1 + 2 * sum(size_of(grp) - 1 for grp in part) for part in PARTS)


def scratch_of():
    vmem = pltpu.VMEM
    shapes = [vmem((ROWS, SNPS), BF16), vmem((ROWS, TRAITS), BF16), vmem((SNPS, TRAITS), F32), vmem((SNPS, 128), F32)]
    for _ in range(2):
        shapes += [vmem((8, TRAITS), F32), vmem((7, 8, TRAITS), F32)]
    shapes += [vmem((2, 8, TRAITS), F32), vmem((7, 8, TRAITS), F32)]
    for part in PARTS:
        sizes = [size_of(grp) for grp in part]
        blk, n = [], PART
        for s in sizes:
            n //= s
            blk.append(n)
        shapes += [
            vmem((sizes[0], 8, 128), F32), vmem((sizes[0] - 1, 8, 128), F32),
            vmem((sizes[0] - 1, blk[0], TRAITS), BF16), vmem((blk[0], TRAITS), F32),
        ]
        shapes += [vmem((s - 1, b, TRAITS), BF16) for s, b in zip(sizes, blk)]
        shapes += [vmem((b, TRAITS), F32) for b in blk[:-1]]
        shapes += [vmem((b, TRAITS), BF16) for b in blk[:-1]]
        shapes += [vmem((*sizes, OWN, TRAITS), BF16)]
    shapes += [
        vmem((ROWS, TRAITS), F32), vmem((256, TRAITS), F32), vmem((256, TRAITS), F32), vmem((256, TRAITS), F32),
        vmem((128, TRAITS), F32), vmem((128, TRAITS), F32), vmem((2, 2, 128, TRAITS), F32),
        vmem((3, 8, 128), F32), vmem((2, 8, 128), F32), vmem((8, 8, 8, 128), F32),
        vmem((2, 8, 16, TRAITS), F32), vmem((8, 16, TRAITS), F32), vmem((7, 16, TRAITS), F32), vmem((16, TRAITS), F32),
        vmem((15, 16, TRAITS), F32), vmem((2, 8, 16, TRAITS), F32),
        pltpu.SemaphoreType.DMA((5,)), pltpu.SemaphoreType.DMA((COPIES,)), pltpu.SemaphoreType.DMA((COPIES,)),
    ]
    return shapes


def finish(gram_ref, stat_ref, proj_ref, basis_ref, fit_ref, cov_ref, score_ref):
    gram = gram_ref[...]
    norm_row, off = stat_ref[0:1, :], stat_ref[1:2, :]
    square = (TRAITS, TRAITS)
    eye = lax.broadcasted_iota(jnp.int32, square, 0) == lax.broadcasted_iota(jnp.int32, square, 1)
    diag_row = jnp.sum(jnp.where(eye, gram, 0.0), axis=0, keepdims=True)
    step_row = norm_row / (diag_row + (SAMPLES / 8.0) * norm_row)
    step_col = jnp.sum(jnp.where(eye, jnp.broadcast_to(step_row, square), 0.0), axis=1, keepdims=True)
    cov = step_col * gram * step_row * (1.0 / SAMPLES)
    cov_ref[...] = cov
    spread = jnp.sum(step_row * step_row * diag_row, axis=1, keepdims=True) * (1.0 / SAMPLES) + 1e-6
    dims1 = (((1,), (1,)), ((), ()))
    loading = lax.dot_general(basis_ref[...], cov, (((1,), (1,)), ((), ())), precision=HIGHEST,
                              preferred_element_type=F32) * (TRAITS / spread)
    high = loading.astype(BF16)
    low = (loading - high.astype(F32)).astype(BF16)
    f = ((proj_ref[...].reshape(ROWS, TRAITS) + off) * step_row).astype(BF16)
    fit_ref[...] = f
    score_ref[...] = (lax.dot_general(high, f, dims1, preferred_element_type=F32)
                      + lax.dot_general(low, f, dims1, preferred_element_type=F32))


def local(genotypes, traits, trait_basis):
    anywhere = pl.BlockSpec(memory_space=pl.ANY)
    inside = pl.BlockSpec(memory_space=pltpu.VMEM)
    gram, stat, proj = pl.pallas_call(
        kernel,
        out_shape=(
            jax.ShapeDtypeStruct((TRAITS, TRAITS), F32),
            jax.ShapeDtypeStruct((8, TRAITS), F32),
            jax.ShapeDtypeStruct((2, 2, 128, TRAITS), F32),
        ),
        in_specs=[anywhere, anywhere],
        out_specs=(inside, inside, anywhere),
        scratch_shapes=scratch_of(),
        compiler_params=pltpu.CompilerParams(
            collective_id=0, has_side_effects=True, vmem_limit_bytes=56 * 2**20),
    )(genotypes, traits)
    fitted, covariance, scores = pl.pallas_call(
        finish,
        out_shape=(
            jax.ShapeDtypeStruct((ROWS, TRAITS), BF16),
            jax.ShapeDtypeStruct((TRAITS, TRAITS), F32),
            jax.ShapeDtypeStruct((RANK, ROWS), F32),
        ),
        in_specs=[inside] * 4,
        out_specs=(inside, inside, inside),
    )(gram, stat, proj, trait_basis.T)
    return fitted, covariance, scores.T


def solution(mesh):
    return jax.shard_map(
        local,
        mesh=mesh,
        in_specs=(P("samp", "snp"), P("samp", None), P()),
        out_specs=(P("samp", None), P(), P("samp", None)),
        check_vma=False,
    )
```

time: 1560 us -> 92.6 us (0.06); the launches traced: 1530 us -> 92.5 us
  waiting for transfers between devices: 1050 us -> 0 us
  blocking collectives: 439 us -> 0 us
  Pallas kernels: 0 us -> 91.8 us
  matrix products: 17.4 us -> 0 us
    psum x3 -> x0, waiting for transfers between devices: 1050 us -> none  [the longest x1 627 us: local(): lax.psum(product - geno_mean[:, None] * trait_local[None, :], 'samp')]
    psum x3 -> x0, blocking collectives: 439 us -> none  [the longest x1 257 us: local(): lax.psum(jnp.sum(genotypes, axis=0, dtype=jnp.float32), 'samp')]
    pallas_call x0 -> x2, Pallas kernels: none -> 91.8 us  [the longest x1 89.1 us: local(): pl.pallas_call(kernel, out_shape=(jax.ShapeDtypeStruct((TRAITS, TRAITS),...]
    dot_general x6 -> x0, matrix products: 17.4 us -> none  [the longest x1 5.9 us: local(): lax.dot_general(genotypes, traits, (((0,), (0,)), ((), ())), preferred_el...]
  transfers between devices with their start and end apart: 3 -> 0, of which waited for: 3 -> 0; matrix products, arithmetic and copies ran while one was open for 0% -> 0% of each run, Pallas kernels for 0% -> 0%
where the time goes in v2:
time: 92.6 us; the launch traced here: 92.5 us
  Pallas kernels  91.8 us (99%)
    pallas_call x1, Pallas kernels, local(): pl.pallas_call(kernel, out_shape=(jax.ShapeDtypeStruct((TRAITS, TRAITS),...  89.1 us
    pallas_call x1, Pallas kernels, local(): pl.pallas_call(finish, out_shape=(jax.ShapeDtypeStruct((ROWS, TRAITS), BF...  2.75 us

profile of v2, /device:TPU:1, one launch (start us, length us, event | category | flops | bytes accessed | tf_op | source)
XLA Modules:
  0.0 92.5 jit_solution(16423735992145263924)
XLA Ops:
  0.6 89.1 %shard_map.58 = (f32[256,256]{1,0:T(8,128)}, f32[8,256]{1,0:T(8,128)}, f32[2,2,128,256]{3,2,1,0:T(8,128)}) custom-call(bf16[512,4096]{1,0:T(8,128)(2,1)} %g_hbm.1, bf16[512,256]{1,0:T(8,128)(2,1)} %t_hbm.1), custom_call_target="tpu_custom_call" | custom-call | tf_op jit(solution)/shard_map/pallas_call | solution.py:402
  89.7 2.8 %shard_map.59 = (bf16[512,256]{1,0:T(8,128)(2,1)}, f32[256,256]{1,0:T(8,128)}, f32[64,512]{1,0:T(8,128)}) custom-call(f32[256,256]{1,0:T(8,128)} %get-tuple-element.9.gram_ref, f32[8,256]{1,0:T(8,128)} %get-tuple-element.10.stat_ref, f32[2,2,128,256]{3,2,1,0:T(8,128)} %get-tuple-element.11.proj_ref, f32[64,256]{1,0:T(8,128)} %bitcast.2), custom_call_target="tpu_custom_call" | custom-call | tf_op jit(solution)/shard_map/pallas_call | solution.py:415

commit v3 on v2

v3 whole, which is shorter than its diff:
```python
import itertools

import jax
import jax.numpy as jnp
from jax import lax
from jax.experimental import pallas as pl
from jax.experimental.pallas import tpu as pltpu
from jax.sharding import PartitionSpec as P

MESH = pl.DeviceIdType.MESH
F32, BF16 = jnp.float32, jnp.bfloat16
HIGHEST = lax.Precision.HIGHEST
SIZE = {"x": 4, "y": 2, "z": 8, "h": 2}
ROWS, SNPS, TRAITS, RANK = 512, 4096, 256, 64
GROUPS = 64
SAMPLES = GROUPS * ROWS
DIMS0 = (((0,), (0,)), ((), ()))
PLANE, ALONG = ("x", "y"), ("z",)
BLOCKS = ((("y",), ("x",), ALONG), (("x",), ("y",), ALONG), (ALONG, PLANE), (("y",), ("x",), ALONG))
PART = SNPS // len(BLOCKS)
OWN = PART // GROUPS
WIDTH = 128
PARTS = tuple((groups, b, h) for b, groups in enumerate(BLOCKS) for h in range(2))
ORDER = (
    (3, 0), (1, 0), (2, 0), (4, 0), (0, 0), (7, 0), (5, 0), (1, 1), (6, 0), (0, 1), (2, 1), (7, 1),
    (3, 1), (0, 2), (4, 1), (1, 2), (6, 1), (2, 2), (3, 2), (7, 2), (0, 3), (4, 2), (5, 1), (6, 2),
    (1, 3), (2, 3), (3, 3), (0, 4), (6, 3), (1, 4), (7, 3), (5, 2), (2, 4), (3, 4), (4, 3), (0, 5),
    (6, 4), (1, 5), (7, 4), (5, 3), (3, 5), (2, 5), (6, 5), (4, 4), (7, 5), (6, 6), (3, 6), (2, 6),
    (1, 6), (0, 6), (5, 4), (7, 6),
)
SLOTS = {PLANE: (0, 1, 2, 3, 4, 5, 6), ("x",): (1, 3, 5), ("y",): (0,)}


def size_of(group):
    n = 1
    for d in group:
        n *= SIZE[d]
    return n


def dot_rows(a, b):
    return lax.dot_general(a, b, DIMS0, precision=HIGHEST, preferred_element_type=F32)


def kernel(g_hbm, t_hbm, gram_ref, stat_ref, proj_hbm, *scratch):
    it = iter(scratch)
    g, t, raw, gsum = (next(it) for _ in range(4))
    mean, mean_in = {}, {}
    for grp in (PLANE, ALONG):
        mean[grp], mean_in[grp] = next(it), next(it)
    wide, wide_in = next(it), next(it)
    tables = [(next(it), next(it), next(it)) for _ in BLOCKS]
    bufs = []
    for part, _, _ in PARTS:
        b = {"out": next(it), "corr": next(it)}
        b["in"] = [next(it) for _ in part]
        b["acc"] = [None] + [next(it) for _ in part[1:]]
        b["low"] = [None] + [next(it) for _ in part[1:]]
        bufs.append(b)
    p, pb, pb_in, hb, hb_in, full = (next(it) for _ in range(6))
    tile, tile_in, every = next(it), next(it), next(it)
    gt, gc_in, gh_in, gz, gz_in, gall = (next(it) for _ in range(6))
    load_sem, send_sem, recv_sem = next(it), next(it), next(it)

    samp, snp = lax.axis_index("samp"), lax.axis_index("snp")
    me = {"x": lax.rem(samp // 2, 4), "y": lax.rem(samp, 2), "z": samp // 8, "h": snp // 2}
    core = lax.rem(snp, 2)

    def index(group, c=me):
        i = 0
        for d in group:
            i = i * SIZE[d] + c[d]
        return i

    def peers(group):
        for ks in itertools.product(*(range(SIZE[d]) for d in group)):
            if any(ks):
                c = dict(me)
                for d, k in zip(group, ks):
                    c[d] = lax.rem(me[d] + k, SIZE[d])
                yield index(group, c), ((c["z"] * 4 + c["x"]) * 2 + c["y"], c["h"] * 2 + core)

    plane, along = list(peers(PLANE)), list(peers(ALONG))
    layer = list(peers(("x", "y", "h")))
    (_, other_half), = peers(("h",))
    other_core = (samp, me["h"] * 2 + (1 - core))
    met = [dev for _, dev in layer + along] + [other_core]

    barrier = pltpu.get_barrier_semaphore()
    for dev in met:
        pl.semaphore_signal(barrier, inc=1, device_id=dev, device_id_type=MESH)
    t_copy = pltpu.make_async_copy(t_hbm, t, load_sem.at[0])
    t_copy.start()
    g_copies = []
    for i in range(len(BLOCKS)):
        cols = pl.ds(i * PART, PART)
        cp = pltpu.make_async_copy(g_hbm.at[:, cols], g.at[:, cols], load_sem.at[1 + i])
        cp.start()
        g_copies.append(cp)

    count = [0]
    started = []

    def send(src, dst, dev):
        i = count[0]
        count[0] += 1
        cp = pltpu.make_async_remote_copy(
            src_ref=src, dst_ref=dst, send_sem=send_sem.at[i], recv_sem=recv_sem.at[i],
            device_id=dev, device_id_type=MESH)
        cp.start()
        started.append(cp)
        return cp

    def wait(copies):
        for cp in copies:
            cp.wait_recv()

    t_copy.wait()

    def add_rows(i, acc):
        b = t[pl.ds(pl.multiple_of(i * 64, 64), 64), :].astype(F32)
        return acc + jnp.sum(b.reshape(8, 8, TRAITS), axis=0)

    acc = lax.fori_loop(0, ROWS // 64, add_rows, jnp.zeros((8, TRAITS), F32))
    own_mean = jnp.sum(acc, axis=0, keepdims=True) * (1.0 / ROWS)
    for grp in (PLANE, ALONG):
        mean[grp][...] = own_mean
    pl.semaphore_wait(barrier, len(met))
    c_plane = [send(mean[PLANE], mean_in[PLANE].at[k], dev) for k, (_, dev) in enumerate(plane)]
    c_along = [] if all(part[0] != ALONG for part in BLOCKS) else [send(mean[ALONG], mean_in[ALONG].at[k], dev) for k, (_, dev) in enumerate(along)]

    ones_col = jnp.ones((ROWS, 128), BF16)
    ones_row = jnp.ones((8, ROWS), BF16)
    sent = [dict() for _ in PARTS]
    norms = [[], []]
    made, s_sent = set(), {}

    def devices(part, s):
        return {PLANE: plane, ALONG: along}[part[s]] if part[s] in (PLANE, ALONG) else list(peers(part[s]))

    def blocks(part):
        out, n = [], PART
        for grp in part:
            n //= size_of(grp)
            out.append(n)
        return out

    def centred(r, n, h):
        cols = pl.ds(h * WIDTH, WIDTH)
        return raw[pl.ds(r, n), cols] - gsum[pl.ds(r, n), :] * mean[PLANE][:, cols]

    def make(block):
        part = BLOCKS[block]
        blk = blocks(part)[0]
        s_out, s_in, _ = tables[block]
        g_copies[block].wait()
        for j in range(PART // 512):
            cols = pl.ds(block * PART + j * 512, 512)
            piece = g[:, cols]
            raw[cols, :] = lax.dot_general(piece, t[...], DIMS0, preferred_element_type=F32)
            gsum[cols, :] = lax.dot_general(piece, ones_col, DIMS0, preferred_element_type=F32)
            sums = jnp.dot(ones_row, piece, preferred_element_type=F32)[:1]
            for q in range(4):
                lane = j * 512 + q * 128
                s_out[lane // blk, pl.ds((lane % blk) // 128, 1), :] = sums[:, q * 128:q * 128 + 128]
        s_sent[block] = [send(s_out.at[to], s_in.at[k], dev) for k, (to, dev) in enumerate(devices(part, 0))]

    def first_send(i):
        (part, block, h), b = PARTS[i], bufs[i]
        blk = blocks(part)[0]
        if block not in made:
            made.add(block)
            make(block)
        cps = []
        for k, (to, dev) in enumerate(devices(part, 0)):
            def fill(j, _):
                r = pl.multiple_of(j * 128, 128)
                v = centred(pl.multiple_of(block * PART + to * blk + r, 128), 128, h)
                b["out"][k, pl.ds(r, 128), :] = v.astype(BF16)
                return 0
            lax.fori_loop(0, blk // 128, fill, 0)
            cps.append(send(b["out"].at[k], b["in"][0].at[k], dev))
        sent[i]["rs"] = cps

    def reduce(i, s):
        (part, block, h), b = PARTS[i], bufs[i]
        blk = blocks(part)[s]
        n = size_of(part[s])
        last = s == len(part) - 1
        mine = index(part[s])
        cols = pl.ds(h * WIDTH, WIDTH)
        if s == 0:
            wait(s_sent.pop(block, []))
            grp = part[0]
            if grp == ALONG:
                wait(c_along)
                c_along.clear()
            means, slots = (ALONG, range(7)) if grp == ALONG else (PLANE, SLOTS[grp])
            s_out, s_in, _ = tables[block]
            lines = [s_out.at[mine]] + [s_in.at[k] for k in range(n - 1)]
            sums = jnp.concatenate(
                [jnp.concatenate([ref[pl.ds(q, 1), :] for q in range(blk // 128)], axis=1) for ref in lines]
                + [jnp.zeros((8 - n, blk), F32)] * (n < 8), axis=0)
            gaps = jnp.concatenate(
                [mean[means][:1, cols]] + [mean_in[means][k, :1, cols] for k in slots]
                + [jnp.zeros((8 - n, WIDTH), F32)] * (n < 8), axis=0) - wide[1, :1, cols]
            b["corr"][...] = dot_rows(sums, gaps)
        wait(sent[i]["rs"])
        rows = min(blk, 128)

        def body(j, norm):
            r = pl.multiple_of(j * rows, rows)
            if s == 0:
                v = centred(pl.multiple_of(block * PART + mine * blk + r, rows), rows, h) + b["corr"][pl.ds(r, rows), :]
            else:
                v = b["acc"][s][pl.ds(pl.multiple_of(mine * blk + r, rows), rows), :]
            for k in range(n - 1):
                v = v + b["in"][s][k, pl.ds(r, rows), :].astype(F32)
            if last:
                tables[block][2][(*(index(grp) for grp in part), slice(None), cols)] = v.astype(BF16)
                return norm + jnp.sum(v * v, axis=0, keepdims=True)
            b["acc"][s + 1][pl.ds(r, rows), :] = v
            b["low"][s + 1][pl.ds(r, rows), :] = v.astype(BF16)
            return norm

        norm = jnp.zeros((1, WIDTH), F32)
        if blk == rows:
            norm = body(0, norm)
        else:
            norm = lax.fori_loop(0, blk // rows, body, norm)
        if last:
            norms[h].append(norm)
            gather(i, s)
            return
        nxt = blocks(part)[s + 1]
        sent[i]["rs"] = [
            send(b["low"][s + 1].at[pl.ds(pl.multiple_of(to * nxt, nxt), nxt), :], b["in"][s + 1].at[k], dev)
            for k, (to, dev) in enumerate(devices(part, s + 1))]

    def gather(i, s):
        part, block, h = PARTS[i]
        at = tuple(index(grp) for grp in part[:s + 1]) + (slice(None),) * (len(part) - s)
        piece = tables[block][2].at[(*at, pl.ds(h * WIDTH, WIDTH))]
        sent[i]["ag"] = [send(piece, piece, dev) for _, dev in devices(part, s)]

    def project(i):
        block = PARTS[i][1]
        if block not in ready:
            ready.add(block)
            return
        n = tables[block][2][...].reshape(PART, TRAITS)
        v = jnp.dot(g[:, pl.ds(block * PART, PART)], n, preferred_element_type=F32)
        if not projected:
            p[...] = v
        else:
            p[...] += v
        projected.append(block)

    ready = set()
    projected = []
    for turn, (i, step) in enumerate(ORDER):
        stages = len(PARTS[i][0])
        if step == 0:
            first_send(i)
        elif step <= stages:
            if turn and wide_send:
                wait(wide_send)
                v = wide[0]
                for k in range(7):
                    v = v + wide_in[k]
                wide[1] = v * (1.0 / GROUPS)
                wide_send.clear()
            reduce(i, step - 1)
        else:
            wait(sent[i]["ag"])
            s = 2 * stages - step - 1
            if s >= 0:
                gather(i, s)
            else:
                project(i)
        if turn == 0:
            wait(c_plane)
            v = mean[PLANE][...]
            for k in range(7):
                v = v + mean_in[PLANE][k]
            wide[0] = v
            wide_send = [send(wide.at[0], wide_in.at[k], dev) for k, (_, dev) in enumerate(along)]

    own = jnp.sum(p[...], axis=0, keepdims=True) * (1.0 / ROWS)
    lines = [own[:, :128], own[:, 128:]]
    for h in range(2):
        norm = norms[h][0]
        for v in norms[h][1:]:
            norm = norm + v
        lines.append(norm)
    tile[0] = jnp.concatenate(lines, axis=0)

    def rows_at(c, h):
        return pl.ds(pl.multiple_of(c * 256 + h * 128, 128), 128)

    halves = (1 - me["h"], me["h"])
    c1 = []
    for j, h in enumerate(halves):
        pb[j] = p[rows_at(1 - core, h), :] - own
        c1.append(send(pb.at[j], pb_in.at[j], other_core))
    c1.append(send(tile.at[0], tile_in.at[0], other_core))
    wait(c1[:1])
    hb[...] = (p[rows_at(core, halves[0]), :] - own + pb_in[0]).astype(BF16)
    c2 = [send(hb, hb_in, other_half)]
    wait(c1[1:])
    tile[1] = tile[0] + tile_in[0]
    c2.append(send(tile.at[1], tile_in.at[1], other_half))
    near = p[rows_at(core, halves[1]), :] - own + pb_in[1]
    wait(c2[:1])
    mine = near + hb_in[...].astype(F32)
    full[core, me["h"]] = mine
    c3 = [send(full.at[core, me["h"]], full.at[core, me["h"]], other_half)]

    for c in (1 - core, core):
        cols = full[core, me["h"], :, pl.ds(pl.multiple_of(c * 128, 128), 128)]
        gt[c] = dot_rows(cols, mine).reshape(16, 8, TRAITS)
        if c is not core:
            g1 = [send(gt.at[c], gc_in, other_core)]
    wait(c2[1:])
    tile[2] = tile[1] + tile_in[1]
    spot = index(PLANE)
    every[me["z"], spot] = tile[2]
    m1 = [send(every.at[me["z"], spot], every.at[me["z"], spot], dev) for _, dev in plane]
    wait(g1)
    gc_in[...] = gc_in[...] + gt[core]
    g2 = [send(gc_in.at[to], gh_in.at[k], dev) for k, (to, dev) in enumerate(layer)]
    wait(m1)
    m2 = [send(every.at[me["z"]], every.at[me["z"]], dev) for _, dev in along]
    wait(g2)
    mid = index(("x", "y", "h"))
    v = gc_in[mid]
    for k in range(15):
        v = v + gh_in[k]
    gz[...] = v
    g3 = [send(gz, gz_in.at[k], dev) for k, (_, dev) in enumerate(along)]
    wait(g3)
    v = gz[...]
    for k in range(7):
        v = v + gz_in[k]
    gall[core, mid] = v
    piece = gall.at[core, mid]
    g4 = [send(piece, piece, dev) for _, dev in layer]
    wait(c3)
    c4 = [send(full.at[core], full.at[core], other_core)]
    wait(c4)
    proj_copy = pltpu.make_async_copy(full, proj_hbm, load_sem.at[0])
    proj_copy.start()
    wait(g4)
    g5 = [send(gall.at[core], gall.at[core], other_core)]
    wait(m2)
    means = jnp.concatenate([every[:, :, r, :].reshape(GROUPS, 128) for r in range(2)], axis=1)
    norm = jnp.concatenate(
        [jnp.sum(every[:, :, r, :].reshape(GROUPS, 128), axis=0, keepdims=True) for r in (2, 3)], axis=1)
    centre = jnp.sum(means, axis=0, keepdims=True) * (1.0 / GROUPS)
    gap = means - centre
    between = dot_rows(gap, gap) * float(ROWS)
    off = jnp.concatenate([tile[2, 0:1], tile[2, 1:2]], axis=1) - centre
    stat_ref[...] = jnp.concatenate([norm, off, jnp.zeros((6, TRAITS), F32)], axis=0)
    wait(g5)
    gram_ref[...] = gall[...].reshape(TRAITS, TRAITS) + between
    for cp in started:
        cp.wait_send()
    proj_copy.wait()
    assert count[0] == COPIES, count[0]


COPIES = 74 + 7 * any(part[0] == ALONG for part in BLOCKS) + sum(
    size_of(part[0]) - 1 + 4 * sum(size_of(grp) - 1 for grp in part) for part in BLOCKS)


def scratch_of():
    vmem = pltpu.VMEM
    shapes = [vmem((ROWS, SNPS), BF16), vmem((ROWS, TRAITS), BF16), vmem((SNPS, TRAITS), F32), vmem((SNPS, 128), F32)]
    for _ in range(2):
        shapes += [vmem((1, TRAITS), F32), vmem((7, 1, TRAITS), F32)]
    shapes += [vmem((2, 1, TRAITS), F32), vmem((7, 1, TRAITS), F32)]
    for part in BLOCKS:
        sizes = [size_of(grp) for grp in part]
        shapes += [vmem((sizes[0], 8, 128), F32), vmem((sizes[0] - 1, 8, 128), F32), vmem((*sizes, OWN, TRAITS), BF16)]
    for part, _, _ in PARTS:
        sizes = [size_of(grp) for grp in part]
        blk, n = [], PART
        for s in sizes:
            n //= s
            blk.append(n)
        shapes += [vmem((sizes[0] - 1, blk[0], WIDTH), BF16), vmem((blk[0], WIDTH), F32)]
        shapes += [vmem((s - 1, b, WIDTH), BF16) for s, b in zip(sizes, blk)]
        shapes += [vmem((b, WIDTH), F32) for b in blk[:-1]]
        shapes += [vmem((b, WIDTH), BF16) for b in blk[:-1]]
    shapes += [
        vmem((ROWS, TRAITS), F32), vmem((2, 128, TRAITS), F32), vmem((2, 128, TRAITS), F32),
        vmem((128, TRAITS), BF16), vmem((128, TRAITS), BF16), vmem((2, 2, 128, TRAITS), F32),
        vmem((3, 4, 128), F32), vmem((2, 4, 128), F32), vmem((8, 8, 4, 128), F32),
        vmem((2, 16, 8, TRAITS), F32), vmem((16, 8, TRAITS), F32), vmem((15, 8, TRAITS), F32), vmem((8, TRAITS), F32),
        vmem((7, 8, TRAITS), F32), vmem((2, 16, 8, TRAITS), F32),
        pltpu.SemaphoreType.DMA((5,)), pltpu.SemaphoreType.DMA((COPIES,)), pltpu.SemaphoreType.DMA((COPIES,)),
    ]
    return shapes


def finish(gram_ref, stat_ref, proj_ref, basis_ref, fit_ref, cov_ref, score_ref):
    gram = gram_ref[...]
    norm_row, off = stat_ref[0:1, :], stat_ref[1:2, :]
    square = (TRAITS, TRAITS)
    eye = lax.broadcasted_iota(jnp.int32, square, 0) == lax.broadcasted_iota(jnp.int32, square, 1)
    diag_row = jnp.sum(jnp.where(eye, gram, 0.0), axis=0, keepdims=True)
    step_row = norm_row / (diag_row + (SAMPLES / 8.0) * norm_row)
    step_col = jnp.sum(jnp.where(eye, jnp.broadcast_to(step_row, square), 0.0), axis=1, keepdims=True)
    cov = step_col * gram * step_row * (1.0 / SAMPLES)
    cov_ref[...] = cov
    spread = jnp.sum(step_row * step_row * diag_row, axis=1, keepdims=True) * (1.0 / SAMPLES) + 1e-6
    dims1 = (((1,), (1,)), ((), ()))
    loading = lax.dot_general(basis_ref[...], cov, (((1,), (1,)), ((), ())), precision=HIGHEST,
                              preferred_element_type=F32) * (TRAITS / spread)
    high = loading.astype(BF16)
    low = (loading - high.astype(F32)).astype(BF16)
    f = ((proj_ref[...].reshape(ROWS, TRAITS) + off) * step_row).astype(BF16)
    fit_ref[...] = f
    score_ref[...] = (lax.dot_general(high, f, dims1, preferred_element_type=F32)
                      + lax.dot_general(low, f, dims1, preferred_element_type=F32))


def local(genotypes, traits, trait_basis):
    anywhere = pl.BlockSpec(memory_space=pl.ANY)
    inside = pl.BlockSpec(memory_space=pltpu.VMEM)
    gram, stat, proj = pl.pallas_call(
        kernel,
        out_shape=(
            jax.ShapeDtypeStruct((TRAITS, TRAITS), F32),
            jax.ShapeDtypeStruct((8, TRAITS), F32),
            jax.ShapeDtypeStruct((2, 2, 128, TRAITS), F32),
        ),
        in_specs=[anywhere, anywhere],
        out_specs=(inside, inside, anywhere),
        scratch_shapes=scratch_of(),
        compiler_params=pltpu.CompilerParams(
            collective_id=0, has_side_effects=True, vmem_limit_bytes=56 * 2**20),
    )(genotypes, traits)
    fitted, covariance, scores = pl.pallas_call(
        finish,
        out_shape=(
            jax.ShapeDtypeStruct((ROWS, TRAITS), BF16),
            jax.ShapeDtypeStruct((TRAITS, TRAITS), F32),
            jax.ShapeDtypeStruct((RANK, ROWS), F32),
        ),
        in_specs=[inside] * 4,
        out_specs=(inside, inside, inside),
    )(gram, stat, proj, trait_basis.T)
    return fitted, covariance, scores.T


def solution(mesh):
    return jax.shard_map(
        local,
        mesh=mesh,
        in_specs=(P("samp", "snp"), P("samp", None), P()),
        out_specs=(P("samp", None), P(), P("samp", None)),
        check_vma=False,
    )
```

time: 92.6 us -> 88.6 us (0.957)
  Pallas kernels: 91.8 us -> 87.8 us
    pallas_call x1, Pallas kernels: 89.1 us -> 85.1 us  [local(): pl.pallas_call(kernel, out_shape=(jax.ShapeDtypeStruct((TRAITS, TRAITS),...]
where the time goes in v3:
time: 88.6 us; the launch traced here: 88.5 us
  Pallas kernels  87.8 us (99%)
    pallas_call x1, Pallas kernels, local(): pl.pallas_call(kernel, out_shape=(jax.ShapeDtypeStruct((TRAITS, TRAITS),...  85.1 us
    pallas_call x1, Pallas kernels, local(): pl.pallas_call(finish, out_shape=(jax.ShapeDtypeStruct((ROWS, TRAITS), BF...  2.74 us

profile of v3, /device:TPU:1, one launch (start us, length us, event | category | flops | bytes accessed | tf_op | source)
XLA Modules:
  0.0 88.5 jit_solution(9747625820308758137)
XLA Ops:
  0.6 85.1 %shard_map.58 = (f32[256,256]{1,0:T(8,128)}, f32[8,256]{1,0:T(8,128)}, f32[2,2,128,256]{3,2,1,0:T(8,128)}) custom-call(bf16[512,4096]{1,0:T(8,128)(2,1)} %g_hbm.1, bf16[512,256]{1,0:T(8,128)(2,1)} %t_hbm.1), custom_call_target="tpu_custom_call" | custom-call | tf_op jit(solution)/shard_map/pallas_call | solution.py:431
  85.7 2.7 %shard_map.59 = (bf16[512,256]{1,0:T(8,128)(2,1)}, f32[256,256]{1,0:T(8,128)}, f32[64,512]{1,0:T(8,128)}) custom-call(f32[256,256]{1,0:T(8,128)} %get-tuple-element.9.gram_ref, f32[8,256]{1,0:T(8,128)} %get-tuple-element.10.stat_ref, f32[2,2,128,256]{3,2,1,0:T(8,128)} %get-tuple-element.11.proj_ref, f32[64,256]{1,0:T(8,128)} %bitcast.2), custom_call_target="tpu_custom_call" | custom-call | tf_op jit(solution)/shard_map/pallas_call | solution.py:444

commit v4 on v3

--- a/solution.py
+++ b/solution.py
@@ -86,18 +86,19 @@
     other_core = (samp, me["h"] * 2 + (1 - core))
     met = [dev for _, dev in layer + along] + [other_core]
 
+    t_copy = pltpu.make_async_copy(t_hbm, t, load_sem.at[0])
+    t_copy.start()
+    g_copies = {}
+    for i, step in ORDER:
+        block = PARTS[i][1]
+        if step == 0 and block not in g_copies:
+            cols = pl.ds(block * PART, PART)
+            g_copies[block] = pltpu.make_async_copy(g_hbm.at[:, cols], g.at[:, cols], load_sem.at[1 + block])
+            g_copies[block].start()
+
     barrier = pltpu.get_barrier_semaphore()
     for dev in met:
         pl.semaphore_signal(barrier, inc=1, device_id=dev, device_id_type=MESH)
-    t_copy = pltpu.make_async_copy(t_hbm, t, load_sem.at[0])
-    t_copy.start()
-    g_copies = []
-    for i in range(len(BLOCKS)):
-        cols = pl.ds(i * PART, PART)
-        cp = pltpu.make_async_copy(g_hbm.at[:, cols], g.at[:, cols], load_sem.at[1 + i])
-        cp.start()
-        g_copies.append(cp)
-
     count = [0]
     started = []
 

time: 88.6 us -> 89.2 us (level)
  no operation moved by 1% of the time
where the time goes in v4:
time: 89.2 us; the launch traced here: 89.1 us
  Pallas kernels  88.5 us (99%)
    pallas_call x1, Pallas kernels, local(): pl.pallas_call(kernel, out_shape=(jax.ShapeDtypeStruct((TRAITS, TRAITS),...  85.8 us
    pallas_call x1, Pallas kernels, local(): pl.pallas_call(finish, out_shape=(jax.ShapeDtypeStruct((ROWS, TRAITS), BF...  2.75 us

profile of v4, /device:TPU:1, one launch (start us, length us, event | category | flops | bytes accessed | tf_op | source)
XLA Modules:
  0.0 89.1 jit_solution(14055886043647447030)
XLA Ops:
  0.6 85.8 %shard_map.58 = (f32[256,256]{1,0:T(8,128)}, f32[8,256]{1,0:T(8,128)}, f32[2,2,128,256]{3,2,1,0:T(8,128)}) custom-call(bf16[512,4096]{1,0:T(8,128)(2,1)} %g_hbm.1, bf16[512,256]{1,0:T(8,128)(2,1)} %t_hbm.1), custom_call_target="tpu_custom_call" | custom-call | tf_op jit(solution)/shard_map/pallas_call | solution.py:432
  86.4 2.7 %shard_map.59 = (bf16[512,256]{1,0:T(8,128)(2,1)}, f32[256,256]{1,0:T(8,128)}, f32[64,512]{1,0:T(8,128)}) custom-call(f32[256,256]{1,0:T(8,128)} %get-tuple-element.9.gram_ref, f32[8,256]{1,0:T(8,128)} %get-tuple-element.10.stat_ref, f32[2,2,128,256]{3,2,1,0:T(8,128)} %get-tuple-element.11.proj_ref, f32[64,256]{1,0:T(8,128)} %bitcast.2), custom_call_target="tpu_custom_call" | custom-call | tf_op jit(solution)/shard_map/pallas_call | solution.py:445
